TPU v7x, 256 devices: a whole 4x4x8 slice. The times are simulated.
256 devices in a mesh: row: 64 (over z, y, core), col: 4 (over x).
Axes of the slice: x: 4, y: 4, z: 8, core: 2. Of those that a mesh axis runs over, the one named last changes fastest.
Arguments:
- sigma_anc: float32 [8192, 8192], P('row', 'col'), may hold values from -24 to 80, as said below
- panel_hat: float32 [8192, 4096], P('row', 'col'), may hold values from -0.0625 to 0.0625
- pattern: int32 [64, 64], replicated, may hold values from 0 to 1, as said below
- diag_inverse: float32 [4096], P('col'), may hold values from 0.5 to 4
Outputs:
- sigma_cross: float32 [8192, 4096], P('row', 'col')
- variance: float32 [4096], P('col')
Inputs may be any that keep to these rules, and one draw needn't show every extreme that they name: `pattern`: symmetric; every diagonal block is 1. `sigma_anc`: symmetric.
All inputs are finite; a program needn't handle non-finite values.
Results may differ from a plain program's by a relative error of at most 0.000073.
Values sent between devices are 32-bit elements; how exact they have to be, the bound alone decides.
A program may use at most 128 MiB of HBM per device.

v0:
```python
import jax
import jax.numpy as jnp
from jax import lax
from jax.sharding import PartitionSpec as P


def body(sigma_anc, panel_hat, pattern, diag_inverse):
    sigma_rows = lax.all_gather(sigma_anc, "col", axis=1, tiled=True)
    band_rows = sigma_rows.shape[0]
    ancestors = sigma_rows.shape[1]
    blocks = pattern.shape[0]
    block_width = ancestors // blocks
    row_start = lax.axis_index("row") * band_rows
    global_rows = row_start + lax.iota(jnp.int32, band_rows)
    row_onehot = (
        global_rows[:, None] // block_width == lax.iota(jnp.int32, blocks)[None, :]
    ).astype(jnp.float32)
    row_mask = jnp.dot(row_onehot, pattern.astype(jnp.float32), preferred_element_type=jnp.float32)
    expanded = jnp.broadcast_to(row_mask[:, :, None], (band_rows, blocks, block_width)).reshape(
        band_rows, ancestors
    )
    masked = sigma_rows * expanded
    product = jnp.dot(
        masked,
        lax.all_gather(panel_hat, "row", axis=0, tiled=True),
        precision=lax.Precision.HIGHEST,
        preferred_element_type=jnp.float32,
    )
    sigma_cross = -product
    partial_value = jnp.sum(panel_hat * sigma_cross, axis=0)
    summed = lax.psum(partial_value, "row")
    variance = diag_inverse - summed
    return (sigma_cross, variance)


def solution(mesh):
    in_specs = (P("row", "col"), P("row", "col"), P(), P("col"))
    out_specs = (P("row", "col"), P("col"))
    return jax.shard_map(body, mesh=mesh, in_specs=in_specs, out_specs=out_specs, check_vma=False)
```

profile of v0, /device:TPU:2, one launch (start us, length us, event | category | flops | bytes accessed | tf_op | source)
XLA Modules:
  0.0 369.2 jit_solution(3616185705939488497)
XLA Ops:
  7.2 0.0 copy-start.1
  7.2 0.0 all-gather.3.cloned.1.call-start
  7.2 0.7 all-gather.3.cloned.1.call-update
  7.9 0.0 all-gather.5.cloned.1.call-start
  8.0 0.7 all-gather.5.cloned.1.call-update
  8.7 1.0 fusion.3
  9.6 53.2 %all-gather.3.cloned.1.call-done = f32[128,8192]{1,0:T(8,128)} async-done(((f32[128,2048]{1,0:T(8,128)}), f32[128,8192]{1,0:T(8,128)}) %all-gather.3.cloned.1.call-update) | async-done | bytes 4194320 | tf_op jit(solution)/shard_map/all_gather | solution.py:8
  62.9 145.4 %all-gather.5.cloned.1.call-done = f32[8192,1024]{1,0:T(8,128)} async-done(((f32[128,1024]{1,0:T(8,128)}), f32[8192,1024]{1,0:T(8,128)}) %all-gather.5.cloned.1.call-update) | async-done | bytes 33554448 | tf_op jit(solution)/shard_map/all_gather | solution.py:25
  208.3 0.0 copy-start
  208.3 1.1 broadcast_in_dim.2
  209.4 0.0 copy-done.1
  209.5 1.0 copy-done
  210.5 0.0 copy-start.2
  210.5 25.7 %multiply_reduce_fusion = (f32[1024]{0:T(1024)S(1)}, f32[128,1024]{1,0:T(8,128)}) fusion(f32[128,1024]{1,0:T(8,128)S(1)} %copy-done.1, f32[8192,1024]{1,0:T(8,128)} %all-gather.5.cloned.1.call-done, f32[128,8192]{1,0:T(8,128)S(1)} %copy-done, f32[16,8,64,128]{3,2,1,0:T(8,128)S(1)} %bitcast.9), kind=kOutput, calls=%fused_computation.4 | convolution fusion | flops 12886342656 | bytes 42995712 | tf_op jit(solution)/shard_map/dot_general | solution.py:23
  236.2 125.5 %psum.7 = f32[1024]{0:T(1024)S(1)} all-reduce(f32[1024]{0:T(1024)S(1)} %get-tuple-element.2), channel_id=1, replica_groups=mesh['row'=64,'col'=4] {'row'}, use_global_device_ids=true, to_apply=%region_1.2 | all-reduce | flops 1024 | bytes 8192 | tf_op jit(solution)/shard_map/psum | solution.py:31
  361.7 0.0 copy-done.2
  361.7 0.6 sub.10
  (1 shorter events, 0.0 us)
Async XLA Ops:
  7.2 202.3 %copy-start.1 = (f32[128,1024]{1,0:T(8,128)S(1)}, f32[128,1024]{1,0:T(8,128)}, u32[]{:S(2)}) copy-start(f32[128,1024]{1,0:T(8,128)} %param.5) | copy-start | bytes 1572868
  7.2 55.7 %all-gather.3.cloned.1.call-start = ((), (), s32[]{:S(2)}) async-start(), calls=%async_computation | async-start | bytes 5242880 | tf_op jit(solution)/shard_map/all_gather | solution.py:8
  7.9 200.4 %all-gather.5.cloned.1.call-start = ((), (), s32[]{:S(2)}) async-start(), calls=%async_computation.1 | async-start | bytes 34078720 | tf_op jit(solution)/shard_map/all_gather | solution.py:25
  208.3 2.2 copy-start
  210.5 151.2 %copy-start.2 = (f32[1024]{0:T(1024)S(1)}, f32[1024]{0:T(1024)}, u32[]{:S(2)}) copy-start(f32[1024]{0:T(1024)} %param.7) | copy-start | bytes 12292
Sparse Core Ops, SparseCore 0:
  9.8 53.0 all-gather.2
  65.6 142.6 all-gather.4
where the time goes:
time: 369 us
  waiting for transfers between devices  200 us (54%)
  blocking collectives  126 us (34%)
  matrix products  26.7 us (7%)
  between operations  14.1 us (4%)
    all_gather x1, waiting for transfers between devices, body(): lax.all_gather(panel_hat, 'row', axis=0, tiled=True)  145 us
    psum x1, blocking collectives, body(): summed = lax.psum(partial_value, 'row')  126 us
    all_gather x1, waiting for transfers between devices, body(): sigma_rows = lax.all_gather(sigma_anc, 'col', axis=1, tiled=True)  53.2 us
    dot_general x1, matrix products, body(): jnp.dot(masked, lax.all_gather(panel_hat, 'row', axis=0, tiled=True), pre...  25.7 us
  transfers between devices with their start and end apart: 2, of which 2 were waited for; matrix products, arithmetic and copies ran while one was open for 0% of the time, Pallas kernels for 0%

commit v1 on v0

--- a/solution.py
+++ b/solution.py
@@ -22,7 +22,9 @@
     masked = sigma_rows * expanded
     product = jnp.dot(
         masked,
-        lax.all_gather(panel_hat, "row", axis=0, tiled=True),
+        jnp.concatenate(
+            lax.all_to_all(jnp.stack([panel_hat] * lax.axis_size("row")), "row", 0, 0), axis=0
+        ),
         precision=lax.Precision.HIGHEST,
         preferred_element_type=jnp.float32,
     )

time: 369 us -> 933 us (2.53)
  waiting for transfers between devices: 200 us -> 730 us
  starting transfers between devices: 0.08 us -> 12.5 us
  local copies, waits for them, and re-layouts: 2.19 us -> 14.3 us
    all_to_all x0 -> x1, waiting for transfers between devices: none -> 676 us  [body(): lax.all_to_all(jnp.stack([panel_hat] * lax.axis_size('row')), 'row', 0, 0)]
    all_gather x1 -> x0, waiting for transfers between devices: 145 us -> none  [body(): lax.all_gather(panel_hat, 'row', axis=0, tiled=True)]
    all_to_all x0 -> x1, starting transfers between devices: none -> 12.5 us  [body(): lax.all_to_all(jnp.stack([panel_hat] * lax.axis_size('row')), 'row', 0, 0)]
    another operation x0 -> x1, local copies, waits for them, and re-layouts: none -> 12.1 us  [body(): jnp.stack([panel_hat] * lax.axis_size('row'))]
    psum x1, blocking collectives: 126 us -> 135 us  [body(): summed = lax.psum(partial_value, 'row')]
where the time goes in v1:
time: 933 us; the launch traced here: 932 us
  waiting for transfers between devices  730 us (78%)
  blocking collectives  135 us (14%)
  matrix products  25.9 us (3%)
  local copies, waits for them, and re-layouts  14.3 us (2%)
  between operations  14.1 us (2%)
  starting transfers between devices  12.5 us (1%)
    all_to_all x1, waiting for transfers between devices, body(): lax.all_to_all(jnp.stack([panel_hat] * lax.axis_size('row')), 'row', 0, 0)  676 us
    psum x1, blocking collectives, body(): summed = lax.psum(partial_value, 'row')  135 us
    all_gather x1, waiting for transfers between devices, body(): sigma_rows = lax.all_gather(sigma_anc, 'col', axis=1, tiled=True)  52.9 us
    dot_general x1, matrix products, body(): jnp.dot(masked, jnp.concatenate(lax.all_to_all(jnp.stack([panel_hat] * la...  25.7 us
  transfers between devices with their start and end apart: 2, of which 2 were waited for; matrix products, arithmetic and copies ran while one was open for 0% of the time, Pallas kernels for 0%

profile of v1, /device:TPU:2, one launch (start us, length us, event | category | flops | bytes accessed | tf_op | source)
XLA Modules:
  0.0 932.4 jit_solution(8684928712854991326)
XLA Ops:
  7.2 12.1 %stack.2 = f32[64,128,1024]{2,1,0:T(8,128)} broadcast(f32[128,1024]{1,0:T(8,128)} %param.5), dimensions={1,2} | broadcast | bytes 34078720 | tf_op jit(solution)/shard_map/stack | solution.py:26
  19.2 0.0 copy-start.2
  19.3 12.5 %all-to-all-start = ((f32[64,128,1024]{2,1,0:T(8,128)}), f32[64,128,1024]{2,1,0:T(8,128)}, u32[]{:S(2)}, u32[]{:S(2)}) async-start(f32[64,128,1024]{2,1,0:T(8,128)} %stack.2), calls=%async_computation | async-start | bytes 67108864 | tf_op jit(solution)/shard_map/all_to_all | solution.py:26
  31.8 0.0 copy-start.1
  31.8 0.0 all-gather.2.cloned.1.call-start
  31.8 0.7 all-gather.2.cloned.1.call-update
  32.5 0.0 copy-done.2
  32.5 0.2 fusion.3
  32.7 52.9 %all-gather.2.cloned.1.call-done = f32[128,8192]{1,0:T(8,128)} async-done(((f32[128,2048]{1,0:T(8,128)}), f32[128,8192]{1,0:T(8,128)}) %all-gather.2.cloned.1.call-update) | async-done | bytes 4194320 | tf_op jit(solution)/shard_map/all_gather | solution.py:8
  85.6 676.1 %all-to-all-done = f32[64,128,1024]{2,1,0:T(8,128)} async-done(((f32[64,128,1024]{2,1,0:T(8,128)}), f32[64,128,1024]{2,1,0:T(8,128)}, u32[]{:S(2)}, u32[]{:S(2)}) %all-to-all-start) | async-done | bytes 33554464 | tf_op jit(solution)/shard_map/all_to_all | solution.py:26
  761.7 0.0 copy-start
  761.7 1.1 broadcast_in_dim.2
  762.8 0.0 copy-done.1
  762.8 1.0 copy-done
  763.8 0.0 copy-start.3
  763.8 25.7 %multiply_reduce_fusion = (f32[1024]{0:T(1024)S(1)}, f32[128,1024]{1,0:T(8,128)}) fusion(f32[128,1024]{1,0:T(8,128)S(1)} %copy-done.1, f32[8192,1024]{1,0:T(8,128)} %bitcast, f32[128,8192]{1,0:T(8,128)S(1)} %copy-done, f32[16,8,64,128]{3,2,1,0:T(8,128)S(1)} %bitcast.10), kind=kOutput, calls=%fused_computation.4 | convolution fusion | flops 12886342656 | bytes 42995712 | tf_op jit(solution)/shard_map/dot_general | solution.py:23
  789.6 135.4 %psum.7 = f32[1024]{0:T(1024)S(1)} all-reduce(f32[1024]{0:T(1024)S(1)} %get-tuple-element.2), channel_id=1, replica_groups=mesh['row'=64,'col'=4] {'row'}, use_global_device_ids=true, to_apply=%region_1.2 | all-reduce | flops 1024 | bytes 8192 | tf_op jit(solution)/shard_map/psum | solution.py:33
  925.0 0.0 copy-done.3
  925.0 0.6 sub.10
  (1 shorter events, 0.0 us)
Async XLA Ops:
  19.2 13.3 %copy-start.2 = (s32[64,64]{1,0:T(8,128)S(1)}, s32[64,64]{1,0:T(8,128)}, u32[]{:S(2)}) copy-start(s32[64,64]{1,0:T(8,128)} %param.6) | copy-start | bytes 49156
  19.3 742.4 %all-to-all-start = ((f32[64,128,1024]{2,1,0:T(8,128)}), f32[64,128,1024]{2,1,0:T(8,128)}, u32[]{:S(2)}, u32[]{:S(2)}) async-start(f32[64,128,1024]{2,1,0:T(8,128)} %stack.2), calls=%async_computation | async-start | bytes 67108864 | tf_op jit(solution)/shard_map/all_to_all | solution.py:26
  31.8 731.0 %copy-start.1 = (f32[128,1024]{1,0:T(8,128)S(1)}, f32[128,1024]{1,0:T(8,128)}, u32[]{:S(2)}) copy-start(f32[128,1024]{1,0:T(8,128)} %param.5) | copy-start | bytes 1572868
  31.8 53.8 %all-gather.2.cloned.1.call-start = ((), (), s32[]{:S(2)}) async-start(), calls=%async_computation.1 | async-start | bytes 5242880 | tf_op jit(solution)/shard_map/all_gather | solution.py:8
  761.7 2.2 copy-start
  763.8 161.1 %copy-start.3 = (f32[1024]{0:T(1024)S(1)}, f32[1024]{0:T(1024)}, u32[]{:S(2)}) copy-start(f32[1024]{0:T(1024)} %param.7) | copy-start | bytes 12292
Sparse Core Ops, SparseCore 0:
  34.4 51.1 all-gather.1

commit v2 on v0

--- a/solution.py
+++ b/solution.py
@@ -28,7 +28,7 @@
     )
     sigma_cross = -product
     partial_value = jnp.sum(panel_hat * sigma_cross, axis=0)
-    summed = lax.psum(partial_value, "row")
+    summed = jnp.sum(lax.all_gather(partial_value, "row"), axis=0)
     variance = diag_inverse - summed
     return (sigma_cross, variance)
 

time: 369 us -> 288 us (0.78)
  blocking collectives: 126 us -> 42.3 us
    psum x1 -> x0, blocking collectives: 126 us -> none  [body(): summed = lax.psum(partial_value, 'row')]
    all_gather x0 -> x1, blocking collectives: none -> 42.3 us  [body(): summed = jnp.sum(lax.all_gather(partial_value, 'row'), axis=0)]
where the time goes in v2:
time: 288 us; the launch traced here: 286 us
  waiting for transfers between devices  200 us (69%)
  blocking collectives  42.3 us (15%)
  matrix products  26.7 us (9%)
  between operations  14.1 us (5%)
    all_gather x1, waiting for transfers between devices, body(): lax.all_gather(panel_hat, 'row', axis=0, tiled=True)  145 us
    all_gather x1, waiting for transfers between devices, body(): sigma_rows = lax.all_gather(sigma_anc, 'col', axis=1, tiled=True)  53.2 us
    all_gather x1, blocking collectives, body(): summed = jnp.sum(lax.all_gather(partial_value, 'row'), axis=0)  42.3 us
    dot_general x1, matrix products, body(): jnp.dot(masked, lax.all_gather(panel_hat, 'row', axis=0, tiled=True), pre...  25.7 us
  transfers between devices with their start and end apart: 2, of which 2 were waited for; matrix products, arithmetic and copies ran while one was open for 0% of the time, Pallas kernels for 0%

profile of v2, /device:TPU:2, one launch (start us, length us, event | category | flops | bytes accessed | tf_op | source)
XLA Modules:
  0.0 286.1 jit_solution(8327741578123679377)
XLA Ops:
  7.2 0.0 copy-start.1
  7.2 0.0 all-gather.4.cloned.1.call-start
  7.2 0.7 all-gather.4.cloned.1.call-update
  7.9 0.0 all-gather.6.cloned.1.call-start
  8.0 0.7 all-gather.6.cloned.1.call-update
  8.7 1.0 fusion.3
  9.6 53.2 %all-gather.4.cloned.1.call-done = f32[128,8192]{1,0:T(8,128)} async-done(((f32[128,2048]{1,0:T(8,128)}), f32[128,8192]{1,0:T(8,128)}) %all-gather.4.cloned.1.call-update) | async-done | bytes 4194320 | tf_op jit(solution)/shard_map/all_gather | solution.py:8
  62.9 145.4 %all-gather.6.cloned.1.call-done = f32[8192,1024]{1,0:T(8,128)} async-done(((f32[128,1024]{1,0:T(8,128)}), f32[8192,1024]{1,0:T(8,128)}) %all-gather.6.cloned.1.call-update) | async-done | bytes 33554448 | tf_op jit(solution)/shard_map/all_gather | solution.py:25
  208.3 0.0 copy-start
  208.3 1.1 broadcast_in_dim.2
  209.4 0.0 copy-done.1
  209.5 1.0 copy-done
  210.5 0.0 copy-start.2
  210.5 25.7 %multiply_reduce_fusion = (f32[1024]{0:T(1024)S(1)}, f32[128,1024]{1,0:T(8,128)}) fusion(f32[128,1024]{1,0:T(8,128)S(1)} %copy-done.1, f32[8192,1024]{1,0:T(8,128)} %all-gather.6.cloned.1.call-done, f32[128,8192]{1,0:T(8,128)S(1)} %copy-done, f32[16,8,64,128]{3,2,1,0:T(8,128)S(1)} %bitcast.9), kind=kOutput, calls=%fused_computation.4 | convolution fusion | flops 12886342656 | bytes 42995712 | tf_op jit(solution)/shard_map/dot_general | solution.py:23
  236.2 42.3 %all-gather = f32[65536]{0:T(1024)S(1)} all-gather(f32[1024]{0:T(1024)S(1)} %get-tuple-element.2), channel_id=2, replica_groups=mesh['row'=64,'col'=4] {'row'}, dimensions={0}, use_global_device_ids=true | all-gather | bytes 266240 | tf_op jit(solution)/shard_map/all_gather | solution.py:31
  278.6 0.0 copy-done.2
  278.6 0.6 sub.10
  (3 shorter events, 0.1 us)
Async XLA Ops:
  7.2 202.3 %copy-start.1 = (f32[128,1024]{1,0:T(8,128)S(1)}, f32[128,1024]{1,0:T(8,128)}, u32[]{:S(2)}) copy-start(f32[128,1024]{1,0:T(8,128)} %param.5) | copy-start | bytes 1572868
  7.2 55.7 %all-gather.4.cloned.1.call-start = ((), (), s32[]{:S(2)}) async-start(), calls=%async_computation | async-start | bytes 5242880 | tf_op jit(solution)/shard_map/all_gather | solution.py:8
  7.9 200.4 %all-gather.6.cloned.1.call-start = ((), (), s32[]{:S(2)}) async-start(), calls=%async_computation.1 | async-start | bytes 34078720 | tf_op jit(solution)/shard_map/all_gather | solution.py:25
  208.3 2.2 copy-start
  210.5 68.1 %copy-start.2 = (f32[1024]{0:T(1024)S(1)}, f32[1024]{0:T(1024)}, u32[]{:S(2)}) copy-start(f32[1024]{0:T(1024)} %param.7) | copy-start | bytes 12292
Sparse Core Ops, SparseCore 0:
  9.8 53.0 all-gather.3
  65.6 142.6 all-gather.5
